TPU v7x, 32 devices: a whole 2x2x4 slice. The times are simulated.
32 devices in a mesh: rows: 16 (over z, x, core), freq: 2 (over y).
Axes of the slice: x: 2, y: 2, z: 4, core: 2. Of those that a mesh axis runs over, the one named last changes fastest.
Arguments:
- design: float32 [128, 65536], P('rows'), may hold values from 0.05 to 0.95
- passive: int32 [128, 65536], P('rows'), may hold values 0 or 1
- state: bfloat16 [2, 2, 128, 65536], P(None, 'freq', 'rows'), may hold values from -36 to 36
- adjoint: bfloat16 [2, 2, 128, 65536], P(None, 'freq', 'rows'), may hold values from -36 to 36
- omega_sq: float32 [2], replicated, may hold values from 0.05 to 2
- assign: int32 [2], P('freq'), may hold values from 0 to 1, each once
Outputs:
- gradient: float32 [128, 65536], P('rows')
Inputs may be any that keep to these rules, and one draw needn't show every extreme that they name: `assign`: each of 0 .. 1 appears once.
All inputs are finite; a program needn't handle non-finite values. No bound on the sum of `passive` on one device may be relied on, other than what follows from the above.
Results may differ from a plain program's by a relative error of at most 0.0003.
Values may be sent and summed in bfloat16 or wider, within the bound.
A program may use at most 128 MiB of HBM per device.

v0:
```python
import jax
import jax.numpy as jnp
from jax import lax
from jax.sharding import PartitionSpec as P

RADIUS = 8
sharpness = 8.0
threshold = 0.5
exponent = 3.0
soft_floor = 0.001
loss_factor = 0.2
epsilon = 1e-06
stiff_table = [
    [4.0 / 6, -1.0 / 6, -1.0 / 6, -2.0 / 6],
    [-1.0 / 6, 4.0 / 6, -2.0 / 6, -1.0 / 6],
    [-1.0 / 6, -2.0 / 6, 4.0 / 6, -1.0 / 6],
    [-2.0 / 6, -1.0 / 6, -1.0 / 6, 4.0 / 6],
]
mass_table = [
    [4.0 / 36, 2.0 / 36, 2.0 / 36, 1.0 / 36],
    [2.0 / 36, 4.0 / 36, 1.0 / 36, 2.0 / 36],
    [2.0 / 36, 1.0 / 36, 4.0 / 36, 2.0 / 36],
    [1.0 / 36, 2.0 / 36, 2.0 / 36, 4.0 / 36],
]


def extended(block, sides, width):
    for axis, dim in sides:
        count = lax.axis_size(axis)
        forward = [(i, i + 1) for i in range(count - 1)]
        backward = [(target, source) for source, target in forward]
        low = lax.ppermute(
            lax.slice_in_dim(block, block.shape[dim] - width, None, axis=dim), axis, forward
        )
        high = lax.ppermute(lax.slice_in_dim(block, 0, width, axis=dim), axis, backward)
        block = jnp.concatenate([low, block, high], axis=dim)
    return block


def from_behind(block, axis, distance):
    devices = range(lax.axis_size(axis))
    route = [(i - distance, i) for i in devices if i - distance in devices]
    return lax.ppermute(block, axis, route)


def tap_list():
    return [float(RADIUS + 1 - abs(offset)) for offset in range(-RADIUS, RADIUS + 1)]


def row_pass(padded, count):
    taps = tap_list()
    total = taps[0] * padded[0:count]
    for offset in range(1, 2 * RADIUS + 1):
        total = total + taps[offset] * padded[offset : offset + count]
    return total


def col_pass(field):
    taps = tap_list()
    count = field.shape[1]
    padded = jnp.pad(field, ((0, 0), (RADIUS, RADIUS)))
    total = taps[0] * padded[:, 0:count]
    for offset in range(1, 2 * RADIUS + 1):
        total = total + taps[offset] * padded[:, offset : offset + count]
    return total


def edge_sums(start, count, whole):
    positions = start + jnp.arange(count, dtype=jnp.int32)
    total = jnp.zeros((count,), jnp.float32)
    for offset in range(-RADIUS, RADIUS + 1):
        inside = ((positions + offset >= 0) & (positions + offset < whole)).astype(jnp.float32)
        total = total + float(RADIUS + 1 - abs(offset)) * inside
    return total


def project(tilde, passive):
    bottom = jnp.tanh(sharpness * threshold) + jnp.tanh(sharpness * (1.0 - threshold))
    steep = jnp.tanh(sharpness * (tilde - threshold))
    value = (jnp.tanh(sharpness * threshold) + steep) / bottom
    slope = sharpness * (1.0 - steep * steep) / bottom
    solid = passive > 0
    density = jnp.where(solid, 1.0, value)
    slope = jnp.where(solid, 0.0, slope)
    stiffness = exponent * density * density * (1.0 - soft_floor)
    return (stiffness, slope)


def bilinear(table, left, right):
    total = None
    for row_pos in range(4):
        inner = table[row_pos][0] * right[0]
        for col_pos in range(1, 4):
            inner = inner + table[row_pos][col_pos] * right[col_pos]
        term = left[row_pos] * inner
        total = term if total is None else total + term
    return total


def corners(nodes, below):
    stacked = jnp.concatenate([nodes, below], axis=0)
    right_col = jnp.zeros((stacked.shape[0], 1), stacked.dtype)
    shifted = jnp.concatenate([stacked[:, 1:], right_col], axis=1)
    return (stacked[:-1], shifted[:-1], stacked[1:], shifted[1:])


def element_terms(fields, fields_below, duals, duals_below, stiffness, omega):
    state_real = corners(fields[0], fields_below[0])
    state_imag = corners(fields[1], fields_below[1])
    adjoint_real = corners(duals[0], duals_below[0])
    adjoint_imag = corners(duals[1], duals_below[1])
    elastic = bilinear(stiff_table, adjoint_real, state_real) - bilinear(
        stiff_table, adjoint_imag, state_imag
    )
    damped = bilinear(stiff_table, adjoint_real, state_imag) + bilinear(
        stiff_table, adjoint_imag, state_real
    )
    inertia = bilinear(mass_table, adjoint_real, state_real) - bilinear(
        mass_table, adjoint_imag, state_imag
    )
    return stiffness * (elastic - loss_factor * damped) - omega * inertia


def shards(design, passive, state, adjoint, omega_sq, assign):
    slab_rows, width = design.shape
    whole_rows = slab_rows * lax.axis_size("rows")
    top = lax.axis_index("rows") * slab_rows
    weight_sum = (
        edge_sums(top, slab_rows, whole_rows)[:, None] * edge_sums(0, width, width)[None, :]
    )
    padded = extended(design, (("rows", 0),), RADIUS)
    tilde = col_pass(row_pass(padded, slab_rows)) / weight_sum
    stiffness, slope = project(tilde, passive)
    factor = slope / weight_sum
    below_state, below_adjoint = from_behind((state[:, :, :1, :], adjoint[:, :, :1, :]), "rows", -1)
    table = jnp.arange(omega_sq.shape[0], dtype=jnp.int32)
    picked = (assign[:, None] == table[None, :]).astype(jnp.float32)
    omegas = jnp.sum(picked * omega_sq[None, :], axis=1)

    def accumulate(slot, total):
        fields = lax.dynamic_index_in_dim(state, slot, 1, keepdims=False).astype(jnp.float32)
        duals = lax.dynamic_index_in_dim(adjoint, slot, 1, keepdims=False).astype(jnp.float32)
        fields_below = lax.dynamic_index_in_dim(below_state, slot, 1, keepdims=False).astype(
            jnp.float32
        )
        duals_below = lax.dynamic_index_in_dim(below_adjoint, slot, 1, keepdims=False).astype(
            jnp.float32
        )
        omega = lax.dynamic_index_in_dim(omegas, slot, 0, keepdims=False)
        return total + element_terms(fields, fields_below, duals, duals_below, stiffness, omega)

    local = lax.fori_loop(0, state.shape[1], accumulate, jnp.zeros((slab_rows, width), jnp.float32))
    share = lax.psum_scatter(local, "freq", scatter_dimension=1, tiled=True)
    piece_cols = share.shape[1]
    start = lax.axis_index("freq") * piece_cols
    spread = share * lax.dynamic_slice_in_dim(factor, start, piece_cols, 1)
    padded_back = extended(spread, (("rows", 0),), RADIUS)
    rowed = row_pass(padded_back, slab_rows)
    joined = lax.all_gather(rowed, "freq", axis=1, tiled=True)
    back = col_pass(joined)
    total = lax.psum(jnp.sum(back * back), "rows")
    return back * lax.rsqrt(total / (whole_rows * width) + epsilon)


def solution(mesh):
    return jax.shard_map(
        shards,
        mesh=mesh,
        in_specs=(
            P("rows", None),
            P("rows", None),
            P(None, "freq", "rows", None),
            P(None, "freq", "rows", None),
            P(),
            P("freq"),
        ),
        out_specs=P("rows", None),
        check_vma=False,
    )
```

profile of v0, /device:TPU:0, one launch (start us, length us, event | category | flops | bytes accessed | tf_op | source)
XLA Modules:
  0.0 300.1 jit_solution(13670841534242166203)
XLA Ops:
  6.5 0.0 copy-start.4
  6.5 0.0 reduce-scatter.2.cloned.1.call-start
  6.5 3.9 %collective-permute-start = (f32[8,65536]{1,0:T(8,128)}, f32[8,65536]{1,0:T(8,128)}, u32[]{:S(2)}, u32[]{:S(2)}) collective-permute-start(f32[8,65536]{1,0:T(8,128)} %param.6), channel_id=1, source_target_pairs={{0,2},{2,4},{4,6},{6,8},{8,10},{10,12},{12,14},{14,16},{16,18},{18... | collective-permute-start | bytes 6291464 | tf_op jit(solution)/shard_map/ppermute | solution.py:32
  10.4 1.3 collective-permute-start.1
  11.7 1.9 slice.352
  13.6 0.4 copy.9
  14.0 1.3 collective-permute-start.2
  15.3 1.9 slice.358
  17.2 1.1 copy.10
  18.3 0.0 copy-start.5
  18.3 1.4 collective-permute-start.3
  19.7 0.0 copy-done.4
  19.7 0.3 convert_element_type.103
  20.0 0.0 copy-done.5
  20.0 0.3 convert_element_type.102
  20.3 1.6 slice_bitcast_fusion.2
  21.9 0.0 copy-start.9
  21.9 2.2 slice_bitcast_fusion.3
  24.8 0.0 copy-start.1
  24.8 0.0 copy-done.9
  24.8 0.6 fusion.172
  25.4 0.0 collective-permute-done.2
  25.4 0.2 convert_element_type.104
  25.6 0.4 slice_bitcast_fusion.7
  26.0 0.0 collective-permute-done.3
  26.0 1.1 convert_element_type.105
  27.1 0.4 slice_bitcast_fusion.6
  27.6 0.0 copy-start.6
  27.6 0.0 copy-start.7
  27.6 0.0 copy-done.1
  27.6 0.0 copy-start
  27.6 6.6 %slice_maximum_fusion = (f32[9,65535]{1,0:T(8,128)}, f32[9,65535]{1,0:T(8,128)}) fusion(f32[1,65536]{1,0:T(1,128)S(1)} %get-tuple-element.46, f32[8,65536]{1,0:T(8,128)} %get-tuple-element.36, f32[1,65536]{1,0:T(1,128)S(1)} %get-tuple-element.45, f32[8,65536]{1,0:T(8,128)S(1)} %copy-done.1), kind=kLoop, calls=%fused_computation | loop fusion | flops 1179630 | bytes 9437112 | tf_op jit(solution)/shard_map/while/body/eval_jaxpr/concatenate | solution.py:101
  34.2 0.0 copy-done.6
  34.2 0.0 copy-done.7
  34.2 0.0 copy-done
  34.2 4.9 %slice_maximum_fusion.1 = (f32[9,65535]{1,0:T(8,128)}, f32[9,65535]{1,0:T(8,128)}) fusion(f32[1,65536]{1,0:T(1,128)S(1)} %get-tuple-element.44, f32[8,65536]{1,0:T(8,128)S(1)} %copy-done, f32[1,65536]{1,0:T(1,128)S(1)} %get-tuple-element.43, f32[8,65536]{1,0:T(8,128)S(1)} %get-tuple-element.38), kind=kLoop, calls=%fused_computation.1 | loop fusion | flops 1179630 | bytes 9437112 | tf_op jit(solution)/shard_map/while/body/eval_jaxpr/concatenate | solution.py:101
  39.1 0.0 copy-start.2
  39.1 0.0 collective-permute-done
  39.1 1.9 constant_dynamic-update-slice_fusion.1
  41.0 0.3 copy-done.2
  41.3 0.3 constant_dynamic-update-slice_fusion
  41.6 0.0 collective-permute-done.1
  41.6 1.7 constant_dynamic-update-slice_fusion.2
  43.3 6.9 %fusion.4 = f32[8,65536]{1,0:T(8,128)} fusion(f32[8,65536]{1,0:T(8,128)} %collective-permute-done.1, f32[16,65536]{1,0:T(8,128)S(1)} %constant_dynamic-update-slice_fusion.2, f32[16,65536]{1,0:T(8,128)S(1)} %get-tuple-element.41, f32[8,65536]{1,0:T(8,128)} %collective-permute-done, f32[8,65536]{1,0:T(8,128)} %param.6), kind=kLoop, calls=%fused_computation.67 | loop fusion | flops 16252928 | bytes 37748736 | tf_op jit(solution)/shard_map/add | solution.py:54
  50.2 46.0 %fusion.2 = (f32[8,65536]{1,0:T(8,128)}, f32[8,65536]{1,0:T(8,128)}, pred[8,65536]{1,0:T(8,128)(4,1)}) fusion(f32[8,65536]{1,0:T(8,128)} %get-tuple-element.40, f32[8,65536]{1,0:T(8,128)} %get-tuple-element.36, f32[8,65536]{1,0:T(8,128)S(1)} %get-tuple-element.38, f32[8,65536]{1,0:T(8,128)} %get-tuple-element.26, f32[1,65536]{1,0:T(1,128)} %copy-done.7, ...), kind=kLoop, calls=%fused_computation.56 | loop fusion | flops 100663296 | bytes 28049300 | tf_op jit(solution)/shard_map/while/body/eval_jaxpr/sub | solution.py:121
  96.2 0.0 copy-start.3
  96.2 0.0 copy-start.8
  96.2 0.0 reduce-scatter.2.cloned.1.call-update
  96.2 0.0 all-gather.2.cloned.1.call-start
  96.3 1.5 broadcast_multiply_fusion.1
  97.8 69.1 %reduce-scatter.2.cloned.1.call-done = f32[8,32768]{1,0:T(8,128)} async-done(((f32[8,65536]{1,0:T(8,128)}), f32[8,32768]{1,0:T(8,128)}) %reduce-scatter.2.cloned.1.call-update) | async-done | bytes 1048592 | tf_op jit(solution)/shard_map/reduce_scatter | solution.py:153
  166.9 0.0 copy-done.3
  166.9 0.0 copy-done.8
  166.9 1.9 fusion.104
  168.7 1.3 collective-permute-start.5
  170.0 3.1 %collective-permute-start.4 = (f32[8,32768]{1,0:T(8,128)S(1)}, f32[8,32768]{1,0:T(8,128)S(1)}, u32[]{:S(2)}, u32[]{:S(2)}) collective-permute-start(f32[8,32768]{1,0:T(8,128)S(1)} %fusion.104), channel_id=1, source_target_pairs={{0,2},{2,4},{4,6},{6,8},{8,10},{10,12},{12,14},{14,16},{16,18},{18... | collective-permute-start | bytes 3145736 | tf_op jit(solution)/shard_map/ppermute | solution.py:32
  173.1 0.1 collective-permute-done.5
  173.3 2.1 collective-permute-done.4
  175.3 4.2 %fusion.66 = f32[8,32768]{1,0:T(8,128)} fusion(f32[8,32768]{1,0:T(8,128)S(1)} %collective-permute-done.5, f32[8,32768]{1,0:T(8,128)S(1)} %fusion.104, f32[8,32768]{1,0:T(8,128)S(1)} %collective-permute-done.4), kind=kLoop, calls=%fused_computation.159 | loop fusion | flops 11796480 | bytes 4194304 | tf_op jit(solution)/shard_map/add | solution.py:54
  179.6 0.0 all-gather.2.cloned.1.call-update
  179.6 53.8 %all-gather.2.cloned.1.call-done = f32[8,65536]{1,0:T(8,128)} async-done(((f32[8,32768]{1,0:T(8,128)}), f32[8,65536]{1,0:T(8,128)}) %all-gather.2.cloned.1.call-update) | async-done | bytes 2097168 | tf_op jit(solution)/shard_map/all_gather | solution.py:159
  233.4 24.1 %multiply_reduce_fusion = (f32[]{:T(128)}, f32[8,65536]{1,0:T(8,128)S(1)}) fusion(f32[8,65536]{1,0:T(8,128)} %all-gather.2.cloned.1.call-done), kind=kLoop, calls=%fused_computation.95 | loop fusion | flops 17301504 | bytes 4194308 | tf_op jit(solution)/shard_map/reduce_sum | solution.py:161
  257.5 33.6 %psum.7 = f32[]{:T(128)} all-reduce(f32[]{:T(128)} %get-tuple-element.21), channel_id=1, replica_groups=mesh['rows'=16,'freq'=2] {'rows'}, use_global_device_ids=true, to_apply=%region_3.4 | all-reduce | flops 1 | bytes 8 | tf_op jit(solution)/shard_map/psum | solution.py:161
  291.8 1.5 broadcast_multiply_fusion
  (2 shorter events, 0.0 us)
Async XLA Ops:
  6.5 13.2 %copy-start.4 = (bf16[2,1,8,65536]{3,2,1,0:T(8,128)(2,1)S(1)}, bf16[2,1,8,65536]{3,2,1,0:T(8,128)(2,1)}, u32[]{:S(2)}) copy-start(bf16[2,1,8,65536]{3,2,1,0:T(8,128)(2,1)} %param.8) | copy-start | bytes 6291460
  6.5 160.3 %reduce-scatter.2.cloned.1.call-start = ((), (), s32[]{:S(2)}) async-start(), calls=%async_computation.1 | async-start | bytes 3145728 | tf_op jit(solution)/shard_map/reduce_scatter | solution.py:153
  6.5 32.5 %collective-permute-start = (f32[8,65536]{1,0:T(8,128)}, f32[8,65536]{1,0:T(8,128)}, u32[]{:S(2)}, u32[]{:S(2)}) collective-permute-start(f32[8,65536]{1,0:T(8,128)} %param.6), channel_id=1, source_target_pairs={{0,2},{2,4},{4,6},{6,8},{8,10},{10,12},{12,14},{14,16},{16,18},{18... | collective-permute-start | bytes 6291464 | tf_op jit(solution)/shard_map/ppermute | solution.py:32
  10.4 31.2 %collective-permute-start.1 = (f32[8,65536]{1,0:T(8,128)}, f32[8,65536]{1,0:T(8,128)}, u32[]{:S(2)}, u32[]{:S(2)}) collective-permute-start(f32[8,65536]{1,0:T(8,128)} %param.6), channel_id=1, source_target_pairs={{2,0},{4,2},{6,4},{8,6},{10,8},{12,10},{14,12},{16,14},{18,16},{20... | collective-permute-start | bytes 6291464 | tf_op jit(solution)/shard_map/ppermute | solution.py:35
  14.0 11.4 %collective-permute-start.2 = (bf16[2,1,1,65536]{3,0,2,1:T(2,128)(2,1)S(1)}, bf16[2,1,1,65536]{3,0,2,1:T(2,128)(2,1)S(1)}, u32[]{:S(2)}, u32[]{:S(2)}) collective-permute-start(bf16[2,1,1,65536]{3,0,2,1:T(2,128)(2,1)S(1)} %copy.9), channel_id=1, source_target_pairs={{2,0},{4,2},{6,4},{8,6},{10,8},{12,10},{14,12},{16,14},{18,16},{20... | collective-permute-start | bytes 786440 | tf_op jit(solution)/shard_map/ppermute | solution.py:43
  18.3 1.7 copy-start.5
  18.3 7.7 %collective-permute-start.3 = (bf16[2,1,1,65536]{3,0,2,1:T(2,128)(2,1)}, bf16[2,1,1,65536]{3,0,2,1:T(2,128)(2,1)}, u32[]{:S(2)}, u32[]{:S(2)}) collective-permute-start(bf16[2,1,1,65536]{3,0,2,1:T(2,128)(2,1)} %copy.10), channel_id=1, source_target_pairs={{2,0},{4,2},{6,4},{8,6},{10,8},{12,10},{14,12},{16,14},{18,16},{20... | collective-permute-start | bytes 786440 | tf_op jit(solution)/shard_map/ppermute | solution.py:43
  21.9 2.9 copy-start.9
  24.8 2.8 copy-start.1
  27.6 6.7 %copy-start.6 = (f32[1,65536]{1,0:T(1,128)}, f32[1,65536]{1,0:T(1,128)S(1)}, u32[]{:S(2)}) copy-start(f32[1,65536]{1,0:T(1,128)S(1)} %get-tuple-element.45) | copy-start | bytes 786436
  27.6 6.7 %copy-start.7 = (f32[1,65536]{1,0:T(1,128)}, f32[1,65536]{1,0:T(1,128)S(1)}, u32[]{:S(2)}) copy-start(f32[1,65536]{1,0:T(1,128)S(1)} %get-tuple-element.46) | copy-start | bytes 786436
  27.6 6.6 %copy-start = (f32[8,65536]{1,0:T(8,128)S(1)}, f32[8,65536]{1,0:T(8,128)}, u32[]{:S(2)}) copy-start(f32[8,65536]{1,0:T(8,128)} %get-tuple-element.40) | copy-start | bytes 6291460
  39.1 2.2 copy-start.2
  96.2 70.7 %copy-start.3 = (f32[8,65536]{1,0:T(8,128)S(1)}, f32[8,65536]{1,0:T(8,128)}, u32[]{:S(2)}) copy-start(f32[8,65536]{1,0:T(8,128)} %get-tuple-element.24) | copy-start | bytes 6291460
  96.2 70.7 %copy-start.8 = (pred[8,65536]{1,0:T(8,128)(4,1)S(1)}, pred[8,65536]{1,0:T(8,128)(4,1)}, u32[]{:S(2)}) copy-start(pred[8,65536]{1,0:T(8,128)(4,1)} %get-tuple-element.25) | copy-start | bytes 1572868
  96.2 137.2 %all-gather.2.cloned.1.call-start = ((), (), s32[]{:S(2)}) async-start(), calls=%async_computation.2 | async-start | bytes 3145728 | tf_op jit(solution)/shard_map/all_gather | solution.py:159
  168.7 4.6 %collective-permute-start.5 = (f32[8,32768]{1,0:T(8,128)S(1)}, f32[8,32768]{1,0:T(8,128)S(1)}, u32[]{:S(2)}, u32[]{:S(2)}) collective-permute-start(f32[8,32768]{1,0:T(8,128)S(1)} %fusion.104), channel_id=1, source_target_pairs={{2,0},{4,2},{6,4},{8,6},{10,8},{12,10},{14,12},{16,14},{18,16},{20... | collective-permute-start | bytes 3145736 | tf_op jit(solution)/shard_map/ppermute | solution.py:35
  170.0 5.3 %collective-permute-start.4 = (f32[8,32768]{1,0:T(8,128)S(1)}, f32[8,32768]{1,0:T(8,128)S(1)}, u32[]{:S(2)}, u32[]{:S(2)}) collective-permute-start(f32[8,32768]{1,0:T(8,128)S(1)} %fusion.104), channel_id=1, source_target_pairs={{0,2},{2,4},{4,6},{6,8},{8,10},{10,12},{12,14},{14,16},{16,18},{18... | collective-permute-start | bytes 3145736 | tf_op jit(solution)/shard_map/ppermute | solution.py:32
Sparse Core Ops, SparseCore 0:
  96.3 70.4 reduce-scatter.1
  179.7 53.6 all-gather.1
where the time goes:
time: 301 us; the launch traced here: 300 us
  waiting for transfers between devices  125 us (42%)
  other arithmetic  100 us (33%)
  blocking collectives  33.6 us (11%)
  between operations  15 us (5%)
  local copies, waits for them, and re-layouts  14.1 us (5%)
  starting transfers between devices  12.3 us (4%)
    reduce_scatter x1, waiting for transfers between devices, shards(): share = lax.psum_scatter(local, 'freq', scatter_dimension=1, tiled=True)  69.1 us
    all_gather x1, waiting for transfers between devices, shards(): joined = lax.all_gather(rowed, 'freq', axis=1, tiled=True)  53.8 us
    sub x1, other arithmetic, element_terms(): return stiffness * (elastic - loss_factor * damped) - omega * inertia  46 us
    psum x1, blocking collectives, shards(): total = lax.psum(jnp.sum(back * back), 'rows')  33.6 us
    reduce_sum x1, other arithmetic, shards(): total = lax.psum(jnp.sum(back * back), 'rows')  24.1 us
    concatenate x2, other arithmetic, corners(): stacked = jnp.concatenate([nodes, below], axis=0)  11.5 us
    add x2, other arithmetic, row_pass(): total = total + taps[offset] * padded[offset:offset + count]  11.1 us
    ppermute x2, starting transfers between devices, extended(): lax.ppermute(lax.slice_in_dim(block, block.shape[dim] - width, None, axis...  6.98 us
  transfers between devices with their start and end apart: 8, of which 4 were waited for; matrix products, arithmetic and copies ran while one was open for 9% of the time, Pallas kernels for 0%

commit v1 on v0

--- a/solution.py
+++ b/solution.py
@@ -156,7 +156,7 @@
     spread = share * lax.dynamic_slice_in_dim(factor, start, piece_cols, 1)
     padded_back = extended(spread, (("rows", 0),), RADIUS)
     rowed = row_pass(padded_back, slab_rows)
-    joined = lax.all_gather(rowed, "freq", axis=1, tiled=True)
+    joined = jnp.concatenate(lax.all_gather(rowed, "freq"), axis=1)
     back = col_pass(joined)
     total = lax.psum(jnp.sum(back * back), "rows")
     return back * lax.rsqrt(total / (whole_rows * width) + epsilon)

time: 301 us -> 301 us (level)
  no operation moved by 1% of the time
where the time goes in v1:
time: 301 us; the launch traced here: 300 us
  waiting for transfers between devices  125 us (42%)
  other arithmetic  100 us (33%)
  blocking collectives  33.6 us (11%)
  between operations  15 us (5%)
  local copies, waits for them, and re-layouts  14.1 us (5%)
  starting transfers between devices  12.3 us (4%)
    reduce_scatter x1, waiting for transfers between devices, shards(): share = lax.psum_scatter(local, 'freq', scatter_dimension=1, tiled=True)  69.1 us
    all_gather x1, waiting for transfers between devices, shards(): joined = jnp.concatenate(lax.all_gather(rowed, 'freq'), axis=1)  53.8 us
    sub x1, other arithmetic, element_terms(): return stiffness * (elastic - loss_factor * damped) - omega * inertia  46 us
    psum x1, blocking collectives, shards(): total = lax.psum(jnp.sum(back * back), 'rows')  33.6 us
    reduce_sum x1, other arithmetic, shards(): total = lax.psum(jnp.sum(back * back), 'rows')  24.1 us
    concatenate x2, other arithmetic, corners(): stacked = jnp.concatenate([nodes, below], axis=0)  11.5 us
    add x2, other arithmetic, row_pass(): total = total + taps[offset] * padded[offset:offset + count]  11.1 us
    ppermute x2, starting transfers between devices, extended(): lax.ppermute(lax.slice_in_dim(block, block.shape[dim] - width, None, axis...  6.98 us
  transfers between devices with their start and end apart: 8, of which 4 were waited for; matrix products, arithmetic and copies ran while one was open for 9% of the time, Pallas kernels for 0%

profile of v1, /device:TPU:0, one launch (start us, length us, event | category | flops | bytes accessed | tf_op | source)
XLA Modules:
  0.0 300.1 jit_solution(13670841534242166203)
XLA Ops:
  6.5 0.0 copy-start.4
  6.5 0.0 reduce-scatter.2.cloned.1.call-start
  6.5 3.9 %collective-permute-start = (f32[8,65536]{1,0:T(8,128)}, f32[8,65536]{1,0:T(8,128)}, u32[]{:S(2)}, u32[]{:S(2)}) collective-permute-start(f32[8,65536]{1,0:T(8,128)} %param.6), channel_id=1, source_target_pairs={{0,2},{2,4},{4,6},{6,8},{8,10},{10,12},{12,14},{14,16},{16,18},{18... | collective-permute-start | bytes 6291464 | tf_op jit(solution)/shard_map/ppermute | solution.py:32
  10.4 1.3 collective-permute-start.1
  11.7 1.9 slice.352
  13.6 0.4 copy.9
  14.0 1.3 collective-permute-start.2
  15.3 1.9 slice.358
  17.2 1.1 copy.10
  18.3 0.0 copy-start.5
  18.3 1.4 collective-permute-start.3
  19.7 0.0 copy-done.4
  19.7 0.3 convert_element_type.103
  20.0 0.0 copy-done.5
  20.0 0.3 convert_element_type.102
  20.3 1.6 slice_bitcast_fusion.2
  21.9 0.0 copy-start.9
  21.9 2.2 slice_bitcast_fusion.3
  24.8 0.0 copy-start.1
  24.8 0.0 copy-done.9
  24.8 0.6 fusion.172
  25.4 0.0 collective-permute-done.2
  25.4 0.2 convert_element_type.104
  25.6 0.4 slice_bitcast_fusion.7
  26.0 0.0 collective-permute-done.3
  26.0 1.1 convert_element_type.105
  27.1 0.4 slice_bitcast_fusion.6
  27.6 0.0 copy-start.6
  27.6 0.0 copy-start.7
  27.6 0.0 copy-done.1
  27.6 0.0 copy-start
  27.6 6.6 %slice_maximum_fusion = (f32[9,65535]{1,0:T(8,128)}, f32[9,65535]{1,0:T(8,128)}) fusion(f32[1,65536]{1,0:T(1,128)S(1)} %get-tuple-element.46, f32[8,65536]{1,0:T(8,128)} %get-tuple-element.36, f32[1,65536]{1,0:T(1,128)S(1)} %get-tuple-element.45, f32[8,65536]{1,0:T(8,128)S(1)} %copy-done.1), kind=kLoop, calls=%fused_computation | loop fusion | flops 1179630 | bytes 9437112 | tf_op jit(solution)/shard_map/while/body/eval_jaxpr/concatenate | solution.py:101
  34.2 0.0 copy-done.6
  34.2 0.0 copy-done.7
  34.2 0.0 copy-done
  34.2 4.9 %slice_maximum_fusion.1 = (f32[9,65535]{1,0:T(8,128)}, f32[9,65535]{1,0:T(8,128)}) fusion(f32[1,65536]{1,0:T(1,128)S(1)} %get-tuple-element.44, f32[8,65536]{1,0:T(8,128)S(1)} %copy-done, f32[1,65536]{1,0:T(1,128)S(1)} %get-tuple-element.43, f32[8,65536]{1,0:T(8,128)S(1)} %get-tuple-element.38), kind=kLoop, calls=%fused_computation.1 | loop fusion | flops 1179630 | bytes 9437112 | tf_op jit(solution)/shard_map/while/body/eval_jaxpr/concatenate | solution.py:101
  39.1 0.0 copy-start.2
  39.1 0.0 collective-permute-done
  39.1 1.9 constant_dynamic-update-slice_fusion.1
  41.0 0.3 copy-done.2
  41.3 0.3 constant_dynamic-update-slice_fusion
  41.6 0.0 collective-permute-done.1
  41.6 1.7 constant_dynamic-update-slice_fusion.2
  43.3 6.9 %fusion.4 = f32[8,65536]{1,0:T(8,128)} fusion(f32[8,65536]{1,0:T(8,128)} %collective-permute-done.1, f32[16,65536]{1,0:T(8,128)S(1)} %constant_dynamic-update-slice_fusion.2, f32[16,65536]{1,0:T(8,128)S(1)} %get-tuple-element.41, f32[8,65536]{1,0:T(8,128)} %collective-permute-done, f32[8,65536]{1,0:T(8,128)} %param.6), kind=kLoop, calls=%fused_computation.67 | loop fusion | flops 16252928 | bytes 37748736 | tf_op jit(solution)/shard_map/add | solution.py:54
  50.2 46.0 %fusion.2 = (f32[8,65536]{1,0:T(8,128)}, f32[8,65536]{1,0:T(8,128)}, pred[8,65536]{1,0:T(8,128)(4,1)}) fusion(f32[8,65536]{1,0:T(8,128)} %get-tuple-element.40, f32[8,65536]{1,0:T(8,128)} %get-tuple-element.36, f32[8,65536]{1,0:T(8,128)S(1)} %get-tuple-element.38, f32[8,65536]{1,0:T(8,128)} %get-tuple-element.26, f32[1,65536]{1,0:T(1,128)} %copy-done.7, ...), kind=kLoop, calls=%fused_computation.56 | loop fusion | flops 100663296 | bytes 28049300 | tf_op jit(solution)/shard_map/while/body/eval_jaxpr/sub | solution.py:121
  96.2 0.0 copy-start.3
  96.2 0.0 copy-start.8
  96.2 0.0 reduce-scatter.2.cloned.1.call-update
  96.2 0.0 all-gather.3.cloned.1.call-start
  96.3 1.5 broadcast_multiply_fusion.1
  97.8 69.1 %reduce-scatter.2.cloned.1.call-done = f32[8,32768]{1,0:T(8,128)} async-done(((f32[8,65536]{1,0:T(8,128)}), f32[8,32768]{1,0:T(8,128)}) %reduce-scatter.2.cloned.1.call-update) | async-done | bytes 1048592 | tf_op jit(solution)/shard_map/reduce_scatter | solution.py:153
  166.9 0.0 copy-done.3
  166.9 0.0 copy-done.8
  166.9 1.9 fusion.104
  168.7 1.3 collective-permute-start.5
  170.0 3.1 %collective-permute-start.4 = (f32[8,32768]{1,0:T(8,128)S(1)}, f32[8,32768]{1,0:T(8,128)S(1)}, u32[]{:S(2)}, u32[]{:S(2)}) collective-permute-start(f32[8,32768]{1,0:T(8,128)S(1)} %fusion.104), channel_id=1, source_target_pairs={{0,2},{2,4},{4,6},{6,8},{8,10},{10,12},{12,14},{14,16},{16,18},{18... | collective-permute-start | bytes 3145736 | tf_op jit(solution)/shard_map/ppermute | solution.py:32
  173.1 0.1 collective-permute-done.5
  173.3 2.1 collective-permute-done.4
  175.3 4.2 %fusion.66 = f32[8,32768]{1,0:T(8,128)} fusion(f32[8,32768]{1,0:T(8,128)S(1)} %collective-permute-done.5, f32[8,32768]{1,0:T(8,128)S(1)} %fusion.104, f32[8,32768]{1,0:T(8,128)S(1)} %collective-permute-done.4), kind=kLoop, calls=%fused_computation.159 | loop fusion | flops 11796480 | bytes 4194304 | tf_op jit(solution)/shard_map/add | solution.py:54
  179.6 0.0 all-gather.3.cloned.1.call-update
  179.6 53.8 %all-gather.3.cloned.1.call-done = f32[16,32768]{1,0:T(8,128)} async-done(((f32[8,32768]{1,0:T(8,128)}), f32[16,32768]{1,0:T(8,128)}) %all-gather.3.cloned.1.call-update) | async-done | bytes 2097168 | tf_op jit(solution)/shard_map/all_gather | solution.py:159
  233.4 24.1 %multiply_reduce_fusion = (f32[]{:T(128)}, f32[8,65536]{1,0:T(8,128)S(1)}) fusion(f32[8,65536]{1,0:T(8,128)} %bitcast.23), kind=kLoop, calls=%fused_computation.95 | loop fusion | flops 17301504 | bytes 4194308 | tf_op jit(solution)/shard_map/reduce_sum | solution.py:161
  257.5 33.6 %psum.7 = f32[]{:T(128)} all-reduce(f32[]{:T(128)} %get-tuple-element.21), channel_id=1, replica_groups=mesh['rows'=16,'freq'=2] {'rows'}, use_global_device_ids=true, to_apply=%region_3.4 | all-reduce | flops 1 | bytes 8 | tf_op jit(solution)/shard_map/psum | solution.py:161
  291.8 1.5 broadcast_multiply_fusion
  (2 shorter events, 0.0 us)
Async XLA Ops:
  6.5 13.2 %copy-start.4 = (bf16[2,1,8,65536]{3,2,1,0:T(8,128)(2,1)S(1)}, bf16[2,1,8,65536]{3,2,1,0:T(8,128)(2,1)}, u32[]{:S(2)}) copy-start(bf16[2,1,8,65536]{3,2,1,0:T(8,128)(2,1)} %param.8) | copy-start | bytes 6291460
  6.5 160.3 %reduce-scatter.2.cloned.1.call-start = ((), (), s32[]{:S(2)}) async-start(), calls=%async_computation.1 | async-start | bytes 3145728 | tf_op jit(solution)/shard_map/reduce_scatter | solution.py:153
  6.5 32.5 %collective-permute-start = (f32[8,65536]{1,0:T(8,128)}, f32[8,65536]{1,0:T(8,128)}, u32[]{:S(2)}, u32[]{:S(2)}) collective-permute-start(f32[8,65536]{1,0:T(8,128)} %param.6), channel_id=1, source_target_pairs={{0,2},{2,4},{4,6},{6,8},{8,10},{10,12},{12,14},{14,16},{16,18},{18... | collective-permute-start | bytes 6291464 | tf_op jit(solution)/shard_map/ppermute | solution.py:32
  10.4 31.2 %collective-permute-start.1 = (f32[8,65536]{1,0:T(8,128)}, f32[8,65536]{1,0:T(8,128)}, u32[]{:S(2)}, u32[]{:S(2)}) collective-permute-start(f32[8,65536]{1,0:T(8,128)} %param.6), channel_id=1, source_target_pairs={{2,0},{4,2},{6,4},{8,6},{10,8},{12,10},{14,12},{16,14},{18,16},{20... | collective-permute-start | bytes 6291464 | tf_op jit(solution)/shard_map/ppermute | solution.py:35
  14.0 11.4 %collective-permute-start.2 = (bf16[2,1,1,65536]{3,0,2,1:T(2,128)(2,1)S(1)}, bf16[2,1,1,65536]{3,0,2,1:T(2,128)(2,1)S(1)}, u32[]{:S(2)}, u32[]{:S(2)}) collective-permute-start(bf16[2,1,1,65536]{3,0,2,1:T(2,128)(2,1)S(1)} %copy.9), channel_id=1, source_target_pairs={{2,0},{4,2},{6,4},{8,6},{10,8},{12,10},{14,12},{16,14},{18,16},{20... | collective-permute-start | bytes 786440 | tf_op jit(solution)/shard_map/ppermute | solution.py:43
  18.3 1.7 copy-start.5
  18.3 7.7 %collective-permute-start.3 = (bf16[2,1,1,65536]{3,0,2,1:T(2,128)(2,1)}, bf16[2,1,1,65536]{3,0,2,1:T(2,128)(2,1)}, u32[]{:S(2)}, u32[]{:S(2)}) collective-permute-start(bf16[2,1,1,65536]{3,0,2,1:T(2,128)(2,1)} %copy.10), channel_id=1, source_target_pairs={{2,0},{4,2},{6,4},{8,6},{10,8},{12,10},{14,12},{16,14},{18,16},{20... | collective-permute-start | bytes 786440 | tf_op jit(solution)/shard_map/ppermute | solution.py:43
  21.9 2.9 copy-start.9
  24.8 2.8 copy-start.1
  27.6 6.7 %copy-start.6 = (f32[1,65536]{1,0:T(1,128)}, f32[1,65536]{1,0:T(1,128)S(1)}, u32[]{:S(2)}) copy-start(f32[1,65536]{1,0:T(1,128)S(1)} %get-tuple-element.45) | copy-start | bytes 786436
  27.6 6.7 %copy-start.7 = (f32[1,65536]{1,0:T(1,128)}, f32[1,65536]{1,0:T(1,128)S(1)}, u32[]{:S(2)}) copy-start(f32[1,65536]{1,0:T(1,128)S(1)} %get-tuple-element.46) | copy-start | bytes 786436
  27.6 6.6 %copy-start = (f32[8,65536]{1,0:T(8,128)S(1)}, f32[8,65536]{1,0:T(8,128)}, u32[]{:S(2)}) copy-start(f32[8,65536]{1,0:T(8,128)} %get-tuple-element.40) | copy-start | bytes 6291460
  39.1 2.2 copy-start.2
  96.2 70.7 %copy-start.3 = (f32[8,65536]{1,0:T(8,128)S(1)}, f32[8,65536]{1,0:T(8,128)}, u32[]{:S(2)}) copy-start(f32[8,65536]{1,0:T(8,128)} %get-tuple-element.24) | copy-start | bytes 6291460
  96.2 70.7 %copy-start.8 = (pred[8,65536]{1,0:T(8,128)(4,1)S(1)}, pred[8,65536]{1,0:T(8,128)(4,1)}, u32[]{:S(2)}) copy-start(pred[8,65536]{1,0:T(8,128)(4,1)} %get-tuple-element.25) | copy-start | bytes 1572868
  96.2 137.2 %all-gather.3.cloned.1.call-start = ((), (), s32[]{:S(2)}) async-start(), calls=%async_computation.2 | async-start | bytes 3145728 | tf_op jit(solution)/shard_map/all_gather | solution.py:159
  168.7 4.6 %collective-permute-start.5 = (f32[8,32768]{1,0:T(8,128)S(1)}, f32[8,32768]{1,0:T(8,128)S(1)}, u32[]{:S(2)}, u32[]{:S(2)}) collective-permute-start(f32[8,32768]{1,0:T(8,128)S(1)} %fusion.104), channel_id=1, source_target_pairs={{2,0},{4,2},{6,4},{8,6},{10,8},{12,10},{14,12},{16,14},{18,16},{20... | collective-permute-start | bytes 3145736 | tf_op jit(solution)/shard_map/ppermute | solution.py:35
  170.0 5.3 %collective-permute-start.4 = (f32[8,32768]{1,0:T(8,128)S(1)}, f32[8,32768]{1,0:T(8,128)S(1)}, u32[]{:S(2)}, u32[]{:S(2)}) collective-permute-start(f32[8,32768]{1,0:T(8,128)S(1)} %fusion.104), channel_id=1, source_target_pairs={{0,2},{2,4},{4,6},{6,8},{8,10},{10,12},{12,14},{14,16},{16,18},{18... | collective-permute-start | bytes 3145736 | tf_op jit(solution)/shard_map/ppermute | solution.py:32
Sparse Core Ops, SparseCore 0:
  96.3 70.4 reduce-scatter.1
  179.7 53.6 all-gather.2
